TPU v7x, 32 devices: a whole 2x2x4 slice. The times are simulated.
32 devices in a mesh: ctx: 8 (over y, x, core), fsdp: 4 (over z).
Axes of the slice: x: 2, y: 2, z: 4, core: 2. Of those that a mesh axis runs over, the one named last changes fastest.
Arguments:
- layer_in: bfloat16 [4, 1024, 1600], P('fsdp', 'ctx'), may hold values from -6 to 6
- out_cot: bfloat16 [4, 1024, 1600], P('fsdp', 'ctx'), may hold values from -6 to 6
- first_gain: bfloat16 [1600], P('fsdp'), may hold values from 0.5 to 1.5
- first_bias: bfloat16 [1600], P('fsdp'), may hold values from -3 to 3
- qkv_weight: bfloat16 [1600, 4800], P('fsdp'), may hold values from -0.15625 to 0.15625
- qv_bias: bfloat16 [2, 1600], P(None, 'fsdp'), may hold values from -3 to 3
- out_weight: bfloat16 [1600, 1600], P('fsdp'), may hold values from -0.625 to 0.625
- out_bias: bfloat16 [1600], P('fsdp'), may hold values from -3 to 3
- second_gain: bfloat16 [1600], P('fsdp'), may hold values from 0.5 to 1.5
- second_bias: bfloat16 [1600], P('fsdp'), may hold values from -3 to 3
- fc_weight: bfloat16 [1600, 6400], P('fsdp'), may hold values from -0.15625 to 0.15625
- fc_bias: bfloat16 [6400], P('fsdp'), may hold values from -3 to 3
- proj_weight: bfloat16 [6400, 1600], P(None, 'fsdp'), may hold values from -0.078125 to 0.078125
- proj_bias: bfloat16 [1600], P('fsdp'), may hold values from -3 to 3
Outputs:
- layer_out: bfloat16 [4, 1024, 1600], P('fsdp', 'ctx')
- grad_in: bfloat16 [4, 1024, 1600], P('fsdp', 'ctx')
- grad_first_gain: float32 [1600], P('fsdp')
- grad_first_bias: float32 [1600], P('fsdp')
- grad_qkv_weight: float32 [1600, 4800], P('fsdp')
- grad_qv_bias: float32 [2, 1600], P(None, 'fsdp')
- grad_out_weight: float32 [1600, 1600], P('fsdp')
- grad_out_bias: float32 [1600], P('fsdp')
- grad_second_gain: float32 [1600], P('fsdp')
- grad_second_bias: float32 [1600], P('fsdp')
- grad_fc_weight: float32 [1600, 6400], P('fsdp')
- grad_fc_bias: float32 [6400], P('fsdp')
- grad_proj_weight: float32 [6400, 1600], P(None, 'fsdp')
- grad_proj_bias: float32 [1600], P('fsdp')
All inputs are finite; a program needn't handle non-finite values.
Results may differ from a plain program's by a relative error of at most 0.03.
Values may be sent and summed in bfloat16 or wider, within the bound.
No kernel may reach another device: no remote copies, remote signals or barrier semaphores. Data moves between devices by JAX's collectives and lax.ppermute only.
A program may use at most 512 MiB of HBM per device.

v0:
```python
import math
import jax
import jax.numpy as jnp
from jax import lax
from jax.sharding import PartitionSpec as P

D = 1600
H = 25
HD = 64


def norm_apply(values, norm_gain, norm_bias):
    centre = jnp.mean(values, axis=-1, keepdims=True)
    shifted = values - centre
    spread = jnp.mean(shifted * shifted, axis=-1, keepdims=True)
    return shifted * lax.rsqrt(spread + 1e-05) * norm_gain + norm_bias


def contract_rows(left, right):
    return lax.dot_general(
        left, right, (((0,), (0,)), ((), ())), preferred_element_type=jnp.float32
    )


def contract_cols(left, right):
    return lax.dot_general(
        left, right, (((1,), (1,)), ((), ())), preferred_element_type=jnp.float32
    )


def split_product(form, weights, other):
    upper = weights.astype(jnp.bfloat16)
    lower = (weights - upper.astype(jnp.float32)).astype(jnp.bfloat16)
    return jnp.einsum(form, upper, other, preferred_element_type=jnp.float32) + jnp.einsum(
        form, lower, other, preferred_element_type=jnp.float32
    )


def sweep_blocks(running, piece_rows, handle):
    block_rows = 512
    return lax.fori_loop(
        0,
        piece_rows // block_rows,
        lambda block_index, state_now: handle(state_now, block_index * block_rows, block_rows),
        running,
    )


def on_device(
    layer_in,
    out_cot,
    first_gain,
    first_bias,
    qkv_weight,
    qv_bias,
    out_weight,
    out_bias,
    second_gain,
    second_bias,
    fc_weight,
    fc_bias,
    proj_weight,
    proj_bias,
):
    f32 = jnp.float32
    bf16 = jnp.bfloat16
    factor = 1.0 / math.sqrt(HD)
    gathered = (
        lax.all_gather(first_gain, "fsdp", axis=0, tiled=True),
        lax.all_gather(first_bias, "fsdp", axis=0, tiled=True),
        lax.all_gather(qkv_weight, "fsdp", axis=0, tiled=True),
        lax.all_gather(qv_bias, "fsdp", axis=1, tiled=True),
        lax.all_gather(out_weight, "fsdp", axis=0, tiled=True),
        lax.all_gather(out_bias, "fsdp", axis=0, tiled=True),
        lax.all_gather(second_gain, "fsdp", axis=0, tiled=True),
        lax.all_gather(second_bias, "fsdp", axis=0, tiled=True),
        lax.all_gather(fc_weight, "fsdp", axis=0, tiled=True),
        lax.all_gather(fc_bias, "fsdp", axis=0, tiled=True),
        lax.all_gather(proj_weight, "fsdp", axis=1, tiled=True),
        lax.all_gather(proj_bias, "fsdp", axis=0, tiled=True),
    )
    gain_one = gathered[0].astype(f32)
    bias_one = gathered[1].astype(f32)
    full_qkv = gathered[2]
    bias_qv = gathered[3].astype(f32)
    full_out = gathered[4]
    bias_out = gathered[5].astype(f32)
    gain_two = gathered[6].astype(f32)
    bias_two = gathered[7].astype(f32)
    full_fc = gathered[8]
    bias_fc = gathered[9].astype(f32)
    full_proj = gathered[10]
    bias_proj = gathered[11].astype(f32)
    tokens = layer_in[0].astype(f32)
    local_rows = tokens.shape[0]
    offset = lax.axis_index("ctx") * local_rows
    query_pos = offset + jnp.arange(local_rows, dtype=jnp.int32)
    normed_one = norm_apply(tokens, gain_one, bias_one).astype(bf16)
    projected = jnp.dot(normed_one, full_qkv, preferred_element_type=f32)
    queries = (projected[:, 0:D] + bias_qv[0]).astype(bf16)
    key_rows = projected[:, D : 2 * D].astype(bf16)
    value_rows = (projected[:, 2 * D : 3 * D] + bias_qv[1]).astype(bf16)
    query_heads = queries.reshape(local_rows, H, HD)
    start_state = (
        jnp.full((H, local_rows), -1e30, f32),
        jnp.zeros((H, local_rows), f32),
        jnp.zeros((local_rows, H, HD), f32),
    )
    key_piece = lax.all_gather(key_rows, "ctx", axis=0, tiled=True)
    value_piece = lax.all_gather(value_rows, "ctx", axis=0, tiled=True)

    def forward_step(state_now, begin_row, block_rows):
        row_max, row_total, accum = state_now
        key_block = lax.dynamic_slice_in_dim(key_piece, begin_row, block_rows, 0).reshape(
            block_rows, H, HD
        )
        value_block = lax.dynamic_slice_in_dim(value_piece, begin_row, block_rows, 0).reshape(
            block_rows, H, HD
        )
        key_pos = begin_row + jnp.arange(block_rows, dtype=jnp.int32)
        allowed = (key_pos[None, :] <= query_pos[:, None])[None]
        scores = (
            jnp.einsum("qhd,khd->hqk", query_heads, key_block, preferred_element_type=f32) * factor
        )
        masked = jnp.where(allowed, scores, -1e30)
        new_max = jnp.maximum(row_max, jnp.max(masked, axis=-1))
        weights = jnp.where(allowed, jnp.exp(masked - new_max[:, :, None]), 0.0)
        rescale = jnp.exp(row_max - new_max)
        new_total = row_total * rescale + jnp.sum(weights, axis=-1)
        update = split_product("hqk,khd->qhd", weights, value_block)
        new_accum = accum * rescale.T[:, :, None] + update
        return (new_max, new_total, new_accum)

    row_max, row_total, accum = sweep_blocks(start_state, key_piece.shape[0], forward_step)
    attn_heads = accum / row_total.T[:, :, None]
    log_total = row_max + jnp.log(row_total)
    attn_out = attn_heads.reshape(local_rows, D).astype(bf16)
    resid = tokens + jnp.dot(attn_out, full_out, preferred_element_type=f32) + bias_out
    normed_two = norm_apply(resid, gain_two, bias_two).astype(bf16)
    pre_act = jnp.dot(normed_two, full_fc, preferred_element_type=f32) + bias_fc
    activated = jax.nn.gelu(pre_act, approximate=True).astype(bf16)
    mlp_out = jnp.dot(activated, full_proj, preferred_element_type=f32) + bias_proj
    layer_out = (resid + mlp_out).astype(bf16)[None]
    cotangent = out_cot[0]
    cot_float = cotangent.astype(f32)
    grad_proj = contract_rows(activated, cotangent)
    grad_proj_b = jnp.sum(cot_float, axis=0)
    d_activated = contract_cols(cotangent, full_proj)
    unused_value, gelu_back = jax.vjp(lambda inner: jax.nn.gelu(inner, approximate=True), pre_act)
    d_pre = gelu_back(d_activated)[0].astype(bf16)
    grad_fc = contract_rows(normed_two, d_pre)
    grad_fc_b = jnp.sum(d_pre.astype(f32), axis=0)
    d_norm_two = contract_cols(d_pre, full_fc)
    unused_two, norm_back_two = jax.vjp(norm_apply, resid, gain_two, bias_two)
    d_resid_norm, grad_gain_two, grad_bias_two = norm_back_two(d_norm_two)
    d_resid = cot_float + d_resid_norm
    d_branch = d_resid.astype(bf16)
    mlp_parts = (
        lax.psum_scatter(
            grad_gain_two.astype(jnp.bfloat16), "fsdp", scatter_dimension=0, tiled=True
        ).astype(jnp.float32),
        lax.psum_scatter(
            grad_bias_two.astype(jnp.bfloat16), "fsdp", scatter_dimension=0, tiled=True
        ).astype(jnp.float32),
        lax.psum_scatter(
            grad_fc.astype(jnp.bfloat16), "fsdp", scatter_dimension=0, tiled=True
        ).astype(jnp.float32),
        lax.psum_scatter(
            grad_fc_b.astype(jnp.bfloat16), "fsdp", scatter_dimension=0, tiled=True
        ).astype(jnp.float32),
        lax.psum_scatter(
            grad_proj.astype(jnp.bfloat16), "fsdp", scatter_dimension=1, tiled=True
        ).astype(jnp.float32),
        lax.psum_scatter(
            grad_proj_b.astype(jnp.bfloat16), "fsdp", scatter_dimension=0, tiled=True
        ).astype(jnp.float32),
    )
    mlp_parts = (
        lax.psum(mlp_parts[0].astype(jnp.bfloat16), "ctx").astype(jnp.float32),
        lax.psum(mlp_parts[1].astype(jnp.bfloat16), "ctx").astype(jnp.float32),
        lax.psum(mlp_parts[2].astype(jnp.bfloat16), "ctx").astype(jnp.float32),
        lax.psum(mlp_parts[3].astype(jnp.bfloat16), "ctx").astype(jnp.float32),
        lax.psum(mlp_parts[4].astype(jnp.bfloat16), "ctx").astype(jnp.float32),
        lax.psum(mlp_parts[5].astype(jnp.bfloat16), "ctx").astype(jnp.float32),
    )
    grad_out = contract_rows(attn_out, d_branch)
    grad_out_b = jnp.sum(d_branch.astype(f32), axis=0)
    d_attn = contract_cols(d_branch, full_out).astype(bf16)
    d_attn_heads = d_attn.reshape(local_rows, H, HD)
    delta_cols = jnp.sum(d_attn_heads.astype(f32) * attn_heads, axis=-1)
    delta_rows = delta_cols.T
    seq_rows = lax.axis_size("ctx") * local_rows

    def block_weights(query_block, key_block, lse_block, query_at, key_at):
        allowed = (key_at[None, :] <= query_at[:, None])[None]
        scores = (
            jnp.einsum("qhd,khd->hqk", query_block, key_block, preferred_element_type=f32) * factor
        )
        return jnp.where(allowed, jnp.exp(scores - lse_block[:, :, None]), 0.0)

    buffer_start = jnp.zeros((seq_rows, 2 * D), f32)
    back_start = (jnp.zeros((local_rows, H, HD), f32), buffer_start)
    query_key_piece = lax.all_gather(key_rows, "ctx", axis=0, tiled=True)
    query_value_piece = lax.all_gather(value_rows, "ctx", axis=0, tiled=True)

    def backward_step(state_now, begin_row, block_rows):
        d_query_sum, kv_buffer = state_now
        key_block = lax.dynamic_slice_in_dim(query_key_piece, begin_row, block_rows, 0).reshape(
            block_rows, H, HD
        )
        value_block = lax.dynamic_slice_in_dim(query_value_piece, begin_row, block_rows, 0).reshape(
            block_rows, H, HD
        )
        key_pos = begin_row + jnp.arange(block_rows, dtype=jnp.int32)
        weights = block_weights(query_heads, key_block, log_total, query_pos, key_pos)
        d_weights = jnp.einsum(
            "qhd,khd->hqk", d_attn_heads, value_block, preferred_element_type=f32
        )
        d_scores = (weights * (d_weights - delta_rows[:, :, None])).astype(bf16)
        d_query_sum = (
            d_query_sum
            + jnp.einsum("hqk,khd->qhd", d_scores, key_block, preferred_element_type=f32) * factor
        )
        d_key_block = (
            jnp.einsum("hqk,qhd->khd", d_scores, query_heads, preferred_element_type=f32) * factor
        )
        d_value_block = split_product("hqk,qhd->khd", weights, d_attn_heads)
        zero_col = jnp.zeros((), jnp.int32)
        current = lax.dynamic_slice(kv_buffer, (begin_row, zero_col), (block_rows, 2 * D))
        added = current + jnp.concatenate(
            [d_key_block.reshape(block_rows, D), d_value_block.reshape(block_rows, D)], axis=1
        )
        kv_buffer = lax.dynamic_update_slice(kv_buffer, added, (begin_row, zero_col))
        return (d_query_sum, kv_buffer)

    d_query_sum, kv_buffer = sweep_blocks(back_start, query_key_piece.shape[0], backward_step)
    kv_mine = lax.psum_scatter(
        kv_buffer.astype(jnp.bfloat16), "ctx", scatter_dimension=0, tiled=True
    ).astype(jnp.float32)
    d_kv = kv_mine.astype(bf16)
    d_queries = d_query_sum.reshape(local_rows, D).astype(bf16)
    d_stack = jnp.concatenate([d_queries, d_kv], axis=1)
    grad_qkv = contract_rows(normed_one, d_stack)
    grad_qv_b = jnp.stack(
        [jnp.sum(d_queries.astype(f32), axis=0), jnp.sum(d_kv[:, D : 2 * D].astype(f32), axis=0)]
    )
    d_norm_one = contract_cols(d_stack, full_qkv)
    unused_one, norm_back_one = jax.vjp(norm_apply, tokens, gain_one, bias_one)
    d_in_norm, grad_gain_one, grad_bias_one = norm_back_one(d_norm_one)
    grad_in = (d_resid + d_in_norm).astype(bf16)[None]
    attn_parts = (
        lax.psum_scatter(
            grad_gain_one.astype(jnp.bfloat16), "fsdp", scatter_dimension=0, tiled=True
        ).astype(jnp.float32),
        lax.psum_scatter(
            grad_bias_one.astype(jnp.bfloat16), "fsdp", scatter_dimension=0, tiled=True
        ).astype(jnp.float32),
        lax.psum_scatter(
            grad_qkv.astype(jnp.bfloat16), "fsdp", scatter_dimension=0, tiled=True
        ).astype(jnp.float32),
        lax.psum_scatter(
            grad_qv_b.astype(jnp.bfloat16), "fsdp", scatter_dimension=1, tiled=True
        ).astype(jnp.float32),
        lax.psum_scatter(
            grad_out.astype(jnp.bfloat16), "fsdp", scatter_dimension=0, tiled=True
        ).astype(jnp.float32),
        lax.psum_scatter(
            grad_out_b.astype(jnp.bfloat16), "fsdp", scatter_dimension=0, tiled=True
        ).astype(jnp.float32),
    )
    attn_parts = (
        lax.psum(attn_parts[0].astype(jnp.bfloat16), "ctx").astype(jnp.float32),
        lax.psum(attn_parts[1].astype(jnp.bfloat16), "ctx").astype(jnp.float32),
        lax.psum(attn_parts[2].astype(jnp.bfloat16), "ctx").astype(jnp.float32),
        lax.psum(attn_parts[3].astype(jnp.bfloat16), "ctx").astype(jnp.float32),
        lax.psum(attn_parts[4].astype(jnp.bfloat16), "ctx").astype(jnp.float32),
        lax.psum(attn_parts[5].astype(jnp.bfloat16), "ctx").astype(jnp.float32),
    )
    summed = (
        attn_parts[0],
        attn_parts[1],
        attn_parts[2],
        attn_parts[3],
        attn_parts[4],
        attn_parts[5],
        mlp_parts[0],
        mlp_parts[1],
        mlp_parts[2],
        mlp_parts[3],
        mlp_parts[4],
        mlp_parts[5],
    )
    return (
        layer_out,
        grad_in,
        summed[0],
        summed[1],
        summed[2],
        summed[3],
        summed[4],
        summed[5],
        summed[6],
        summed[7],
        summed[8],
        summed[9],
        summed[10],
        summed[11],
    )


def solution(mesh):
    placed = (
        P("fsdp", "ctx", None),
        P("fsdp", "ctx", None),
        P("fsdp"),
        P("fsdp"),
        P("fsdp", None),
        P(None, "fsdp"),
        P("fsdp", None),
        P("fsdp"),
        P("fsdp"),
        P("fsdp"),
        P("fsdp", None),
        P("fsdp"),
        P(None, "fsdp"),
        P("fsdp"),
    )
    return jax.shard_map(
        on_device,
        mesh=mesh,
        in_specs=placed,
        out_specs=(
            P("fsdp", "ctx", None),
            P("fsdp", "ctx", None),
            P("fsdp"),
            P("fsdp"),
            P("fsdp", None),
            P(None, "fsdp"),
            P("fsdp", None),
            P("fsdp"),
            P("fsdp"),
            P("fsdp"),
            P("fsdp", None),
            P("fsdp"),
            P(None, "fsdp"),
            P("fsdp"),
        ),
        check_vma=False,
    )
```

profile of v0, /device:TPU:0, one launch (start us, length us, event | category | flops | bytes accessed | tf_op | source)
XLA Modules:
  0.0 2622.3 jit_solution(15926004353740264351)
XLA Ops:
  10.0 13.5 all-gather
  25.2 28.7 %all-reduce.17 = (bf16[1600]{0:T(1024)(128)(2,1)S(1)}, bf16[1600]{0:T(1024)(128)(2,1)S(1)}, bf16[1600]{0:T(1024)(128)(2,1)S(1)}, bf16[6400]{0:T(1024)(128)(2,1)S...) all-reduce(bf16[1600]{0:T(1024)(128)(2,1)S(1)} %dynamic-update-slic, ...), channel_id=1, replica_groups=mesh['ctx'=8,'fsdp'=4] {'fsdp'}, use_global_device_ids=true, to_apply=%add.1 | all-reduce | flops 14400 | bytes 57600
  54.5 226.2 %all-gather.8.cloned.1.call-done = bf16[1600,4800]{1,0:T(8,128)(2,1)} async-done(((bf16[400,4800]{1,0:T(8,128)(2,1)}), bf16[1600,4800]{1,0:T(8,128)(2,1)}) %all-gather.8.cloned.1.call-update) | async-done | bytes 15360016 | tf_op jit(solution)/shard_map/all_gather | solution.py:71
  280.8 12.3 fusion.80
  300.1 27.5 %all-gather.12.cloned.1.call-done = bf16[1024,1600]{0,1:T(8,128)(2,1)} async-done(((bf16[128,1600]{0,1:T(8,128)(2,1)}), bf16[1024,1600]{0,1:T(8,128)(2,1)}) %all-gather.12.cloned.1.call-update) | async-done | bytes 3276816 | tf_op jit(solution)/shard_map/all_gather | solution.py:110
  327.6 35.9 %all-gather.10.cloned.1.call-done = bf16[1024,1600]{0,1:T(8,128)(2,1)} async-done(((bf16[128,1600]{0,1:T(8,128)(2,1)}), bf16[1024,1600]{0,1:T(8,128)(2,1)}) %all-gather.10.cloned.1.call-update) | async-done | bytes 3276816 | tf_op jit(solution)/shard_map/all_gather | solution.py:109
  363.5 20.4 while.34
  386.0 78.4 %all-gather.14.cloned.1.call-done = bf16[1600,1600]{1,0:T(8,128)(2,1)} async-done(((bf16[400,1600]{1,0:T(8,128)(2,1)}), bf16[1600,1600]{1,0:T(8,128)(2,1)}) %all-gather.14.cloned.1.call-update) | async-done | bytes 5120016 | tf_op jit(solution)/shard_map/all_gather | solution.py:73
  469.4 343.6 %all-gather.16.cloned.1.call-done = bf16[1600,6400]{1,0:T(8,128)(2,1)} async-done(((bf16[400,6400]{1,0:T(8,128)(2,1)}), bf16[1600,6400]{1,0:T(8,128)(2,1)}) %all-gather.16.cloned.1.call-update) | async-done | bytes 20480016 | tf_op jit(solution)/shard_map/all_gather | solution.py:77
  813.0 12.3 convolution_add_fusion
  825.3 336.6 %all-gather.18.cloned.1.call-done = bf16[6400,1600]{0,1:T(8,128)(2,1)} async-done(((bf16[6400,400]{0,1:T(8,128)(2,1)}), bf16[6400,1600]{0,1:T(8,128)(2,1)}) %all-gather.18.cloned.1.call-update) | async-done | bytes 20480016 | tf_op jit(solution)/shard_map/all_gather | solution.py:79
  1161.9 13.9 fusion.89
  1175.8 13.3 multiply_reduce_fusion
  1198.5 38.6 %while.35 = (s32[]{:T(128)}, f32[128,25,64]{0,2,1:T(8,128)S(1)}, f32[1024,3200]{0,1:T(8,128)}, bf16[1024,1600]{0,1:T(8,128)(2,1)}, bf16[128,25,64]{0,2,1:T(8,128...) while((s32[]{:T(128)}, f32[128,25,64]{0,2,1:T(8,128)S(1)}, ...), condition=%wide.region_12.13_spmd.clone, body=%wide.region_11.12_spmd.clone.sunk | while | flops 1291739776 | bytes 84286680 | solution.py:41
  1260.5 56.5 %reduce-scatter.19.cloned.1.call-done = bf16[128,3200]{1,0:T(8,128)(2,1)} async-done(((bf16[1024,3200]{1,0:T(8,128)(2,1)}), bf16[128,3200]{1,0:T(8,128)(2,1)}) %reduce-scatter.19.cloned.1.call-update) | async-done | bytes 819216
  1328.3 11.7 convolution_convert_fusion
  1354.8 60.5 %reduce-scatter.13.cloned.1.call-done = bf16[400,1600]{1,0:T(8,128)(2,1)} async-done(((bf16[1600,1600]{1,0:T(8,128)(2,1)}), bf16[400,1600]{1,0:T(8,128)(2,1)}) %reduce-scatter.13.cloned.1.call-update) | async-done | bytes 1280016 | tf_op jit(solution)/shard_map/reduce_scatter | solution.py:264
  1415.3 263.4 %reduce-scatter.11.cloned.1.call-done = bf16[400,4800]{1,0:T(8,128)(2,1)} async-done(((bf16[1600,4800]{1,0:T(8,128)(2,1)}), bf16[400,4800]{1,0:T(8,128)(2,1)}) %reduce-scatter.11.cloned.1.call-update) | async-done | bytes 3840016 | tf_op jit(solution)/shard_map/reduce_scatter | solution.py:258
  1678.6 343.0 %reduce-scatter.17.cloned.1.call-done = bf16[6400,400]{0,1:T(8,128)(2,1)} async-done(((bf16[6400,1600]{0,1:T(8,128)(2,1)}), bf16[6400,400]{0,1:T(8,128)(2,1)}) %reduce-scatter.17.cloned.1.call-update) | async-done | bytes 5120016 | tf_op jit(solution)/shard_map/reduce_scatter | solution.py:171
  2021.6 343.3 %reduce-scatter.15.cloned.1.call-done = bf16[400,6400]{1,0:T(8,128)(2,1)} async-done(((bf16[1600,6400]{1,0:T(8,128)(2,1)}), bf16[400,6400]{1,0:T(8,128)(2,1)}) %reduce-scatter.15.cloned.1.call-update) | async-done | bytes 5120016 | tf_op jit(solution)/shard_map/reduce_scatter | solution.py:165
  2377.3 19.8 all-reduce.16
  2400.3 11.6 fusion.50
  2412.9 24.1 all-reduce.14
  2441.7 156.3 %all-reduce.20.cloned.1.call-done = (bf16[400,4800]{1,0:T(8,128)(2,1)}, bf16[400,1600]{1,0:T(8,128)(2,1)}, bf16[400,6400]{1,0:T(8,128)(2,1)}, bf16[6400,400]{0,1:T(8,128)(2,1)}) async-done(((bf16[400,4800]{1,0:T(8,128)(2,1)}, bf16[400,1600]{1,0:T(8,128)(2,1)}, bf16[400,6400]{1,0:T(8,128)(2,1)}, bf16[6400,400]{0,1:T(8,128)(2,1)}), (bf16[400,4800]{1,0:T(8,128)(2,1)}, bf16[400,1600]{1,0:T(8,128)(2,1)}, ...) | async-done | bytes 15360016 | tf_op jit(solution)/shard_map/psum | solution.py:274
  (273 shorter events, 172.0 us)
Async XLA Ops:
  7.3 273.5 %all-gather.8.cloned.1.call-start = ((), (), s32[]{:S(2)}) async-start(), calls=%async_computation.6 | async-start | bytes 19456000 | tf_op jit(solution)/shard_map/all_gather | solution.py:71
  8.0 319.6 %all-gather.12.cloned.1.call-start = ((), (), s32[]{:S(2)}) async-start(), calls=%async_computation.8 | async-start | bytes 3686400 | tf_op jit(solution)/shard_map/all_gather | solution.py:110
  54.0 239.1 %copy-start.26 = (f32[1600]{0:T(1024)}, f32[1600]{0:T(1024)S(1)}, u32[]{:S(2)}) copy-start(f32[1600]{0:T(1024)S(1)} %convert_element_type.234) | copy-start | bytes 19204
  54.0 239.1 %copy-start.22 = (f32[1600]{0:T(1024)}, f32[1600]{0:T(1024)S(1)}, u32[]{:S(2)}) copy-start(f32[1600]{0:T(1024)S(1)} %convert_element_type.233) | copy-start | bytes 19204
  54.3 238.8 %copy-start.32 = (f32[128]{0:T(128)}, f32[128]{0:T(128)S(1)}, u32[]{:S(2)}) copy-start(f32[128]{0:T(128)S(1)} %broadcast_multiply_fusion.1) | copy-start | bytes 1540
  54.5 238.5 %copy-start.51 = (f32[128]{0:T(128)}, f32[128]{0:T(128)S(1)}, u32[]{:S(2)}) copy-start(f32[128]{0:T(128)S(1)} %fusion.61) | copy-start | bytes 1540
  54.5 238.5 %copy-start.38 = (f32[128]{0:T(128)}, f32[128]{0:T(128)S(1)}, u32[]{:S(2)}) copy-start(f32[128]{0:T(128)S(1)} %fusion.75) | copy-start | bytes 1540
  295.7 67.7 %all-gather.10.cloned.1.call-start = ((), (), s32[]{:S(2)}) async-start(), calls=%async_computation.7 | async-start | bytes 3686400 | tf_op jit(solution)/shard_map/all_gather | solution.py:109
  297.7 166.6 %all-gather.14.cloned.1.call-start = ((), (), s32[]{:S(2)}) async-start(), calls=%async_computation.9 | async-start | bytes 6656000 | tf_op jit(solution)/shard_map/all_gather | solution.py:73
  298.3 514.7 %all-gather.16.cloned.1.call-start = ((), (), s32[]{:S(2)}) async-start(), calls=%async_computation.10 | async-start | bytes 25600000 | tf_op jit(solution)/shard_map/all_gather | solution.py:77
  298.9 863.0 %all-gather.18.cloned.1.call-start = ((), (), s32[]{:S(2)}) async-start(), calls=%async_computation.11 | async-start | bytes 25600000 | tf_op jit(solution)/shard_map/all_gather | solution.py:79
  299.5 1017.5 %reduce-scatter.19.cloned.1.call-start = ((), (), s32[]{:S(2)}) async-start(), calls=%async_computation.16 | async-start | bytes 7372800
  300.0 889.1 %copy-start.20 = (f32[1600]{0:T(1024)}, f32[1600]{0:T(1024)S(1)}, u32[]{:S(2)}) copy-start(f32[1600]{0:T(1024)S(1)} %convert_element_type.242) | copy-start | bytes 19204
  300.1 512.9 %copy-start.24 = (f32[1600]{0:T(1024)}, f32[1600]{0:T(1024)S(1)}, u32[]{:S(2)}) copy-start(f32[1600]{0:T(1024)S(1)} %convert_element_type.243) | copy-start | bytes 19204
  469.1 720.0 %copy-start = (f32[128,1600]{0,1:T(8,128)}, f32[128,1600]{0,1:T(8,128)S(1)}, u32[]{:S(2)}) copy-start(f32[128,1600]{0,1:T(8,128)S(1)} %get-tuple-element.486) | copy-start | bytes 2457604
  469.1 720.0 %copy-start.28 = (f32[128]{0:T(128)}, f32[128]{0:T(128)S(1)}, u32[]{:S(2)}) copy-start(f32[128]{0:T(128)S(1)} %broadcast_multiply_fusion) | copy-start | bytes 1540
  469.4 719.8 %copy-start.30 = (f32[128]{0:T(128)}, f32[128]{0:T(128)S(1)}, u32[]{:S(2)}) copy-start(f32[128]{0:T(128)S(1)} %fusion.76) | copy-start | bytes 1540
  469.4 692.5 %copy-start.6 = (bf16[1,128,1600]{1,2,0:T(8,128)(2,1)S(1)}, bf16[1,128,1600]{1,2,0:T(8,128)(2,1)}, u32[]{:S(2)}) copy-start(bf16[1,128,1600]{1,2,0:T(8,128)(2,1)} %param.19) | copy-start | bytes 1228804
  1255.2 160.1 %reduce-scatter.13.cloned.1.call-start = ((), (), s32[]{:S(2)}) async-start(), calls=%async_computation.13 | async-start | bytes 6656000 | tf_op jit(solution)/shard_map/reduce_scatter | solution.py:264
  1260.2 418.5 %reduce-scatter.11.cloned.1.call-start = ((), (), s32[]{:S(2)}) async-start(), calls=%async_computation.12 | async-start | bytes 19456000 | tf_op jit(solution)/shard_map/reduce_scatter | solution.py:258
  1327.3 694.3 %reduce-scatter.17.cloned.1.call-start = ((), (), s32[]{:S(2)}) async-start(), calls=%async_computation.15 | async-start | bytes 25600000 | tf_op jit(solution)/shard_map/reduce_scatter | solution.py:171
  1340.1 1024.8 %reduce-scatter.15.cloned.1.call-start = ((), (), s32[]{:S(2)}) async-start(), calls=%async_computation.14 | async-start | bytes 25600000 | tf_op jit(solution)/shard_map/reduce_scatter | solution.py:165
  1352.2 1059.8 %reduce-scatter.21.cloned.1.call-start = ((), (), s32[]{:S(2)}) async-start(), calls=%async_computation.17 | async-start | bytes 512000
  1354.5 1243.5 %all-reduce.20.cloned.1.call-start = ((), (), s32[]{:S(2)}) async-start(), calls=%async_computation.18 | async-start | bytes 30924800 | tf_op jit(solution)/shard_map/psum | solution.py:274
  (46 other events, 804.4 us)
Sparse Core Ops, SparseCore 0:
  9.7 271.0 all-gather.7
  295.8 31.6 all-gather.11
  330.0 33.3 all-gather.9
  364.9 99.4 all-gather.13
  465.8 347.1 all-gather.15
  814.4 347.4 all-gather.17
  1255.3 61.6 reduce-scatter.18
  1320.0 95.2 reduce-scatter.12
  1417.8 260.8 reduce-scatter.10
  1680.9 340.7 reduce-scatter.16
  2024.1 340.6 reduce-scatter.14
  2367.6 22.1 reduce-scatter.20
  2394.4 203.6 all-reduce.19
where the time goes:
time: 2630 us; the launch traced here: 2620 us
  waiting for transfers between devices  2270 us (86%)
  matrix products  145 us (6%)
  blocking collectives  86.3 us (3%)
  other arithmetic  58.3 us (2%)
  local copies, waits for them, and re-layouts  40.2 us (2%)
    all_gather x1, waiting for transfers between devices, on_device(): lax.all_gather(fc_weight, 'fsdp', axis=0, tiled=True)  344 us
    reduce_scatter x1, waiting for transfers between devices, on_device(): lax.psum_scatter(grad_fc.astype(jnp.bfloat16), 'fsdp', scatter_dimension=...  343 us
    reduce_scatter x1, waiting for transfers between devices, on_device(): lax.psum_scatter(grad_proj.astype(jnp.bfloat16), 'fsdp', scatter_dimensio...  343 us
    all_gather x1, waiting for transfers between devices, on_device(): lax.all_gather(proj_weight, 'fsdp', axis=1, tiled=True)  337 us
    reduce_scatter x1, waiting for transfers between devices, on_device(): lax.psum_scatter(grad_qkv.astype(jnp.bfloat16), 'fsdp', scatter_dimension...  263 us
    all_gather x1, waiting for transfers between devices, on_device(): lax.all_gather(qkv_weight, 'fsdp', axis=0, tiled=True)  226 us
    psum x1, waiting for transfers between devices, on_device(): lax.psum(attn_parts[2].astype(jnp.bfloat16), 'ctx').astype(jnp.float32)  156 us
    all_gather x1, waiting for transfers between devices, on_device(): lax.all_gather(out_weight, 'fsdp', axis=0, tiled=True)  78.4 us
  transfers between devices with their start and end apart: 13, of which 12 were waited for; matrix products, arithmetic and copies ran while one was open for 4% of the time, Pallas kernels for 0%

commit v1 on v0

--- a/solution.py
+++ b/solution.py
@@ -7,6 +7,22 @@
 D = 1600
 H = 25
 HD = 64
+
+
+def ring_gather(x, axis, dim):
+    ways, here, lap = (lax.axis_size(axis), lax.axis_index(axis), x.shape[dim])
+    lengths = [n * ways if d == dim else n for d, n in enumerate(x.shape)]
+    full = lax.dynamic_update_slice_in_dim(jnp.zeros(lengths, x.dtype), x, here * lap, axis=dim)
+    going_up = going_down = x
+    for far in range(1, ways // 2 + 1):
+        going_up = lax.ppermute(going_up, axis, [(d, (d + 1) % ways) for d in range(ways)])
+        full = lax.dynamic_update_slice_in_dim(full, going_up, (here - far) % ways * lap, axis=dim)
+        if 2 * far < ways:
+            going_down = lax.ppermute(going_down, axis, [(d, (d - 1) % ways) for d in range(ways)])
+            full = lax.dynamic_update_slice_in_dim(
+                full, going_down, (here + far) % ways * lap, axis=dim
+            )
+    return full
 
 
 def norm_apply(values, norm_gain, norm_bias):
@@ -70,7 +86,7 @@
         lax.all_gather(first_bias, "fsdp", axis=0, tiled=True),
         lax.all_gather(qkv_weight, "fsdp", axis=0, tiled=True),
         lax.all_gather(qv_bias, "fsdp", axis=1, tiled=True),
-        lax.all_gather(out_weight, "fsdp", axis=0, tiled=True),
+        ring_gather(out_weight, "fsdp", 0),
         lax.all_gather(out_bias, "fsdp", axis=0, tiled=True),
         lax.all_gather(second_gain, "fsdp", axis=0, tiled=True),
         lax.all_gather(second_bias, "fsdp", axis=0, tiled=True),

time: 2630 us -> 2540 us (0.966)
  waiting for transfers between devices: 2270 us -> 2160 us
    ppermute x0 -> x3, waiting for transfers between devices: none -> 81.6 us  [the longest x2 64.2 us: ring_gather(): lax.ppermute(going_up, axis, [(d, (d + 1) % ways) for d in range(ways)])]
    all_gather x1 -> x0, waiting for transfers between devices: 78.4 us -> none  [on_device(): lax.all_gather(out_weight, 'fsdp', axis=0, tiled=True)]
    all_gather x1, waiting for transfers between devices: 344 us -> 296 us  [on_device(): lax.all_gather(fc_weight, 'fsdp', axis=0, tiled=True)]
    all_gather x1, waiting for transfers between devices: 35.9 us -> 0.01 us  [on_device(): key_piece = lax.all_gather(key_rows, 'ctx', axis=0, tiled=True)]
    all_gather x1, waiting for transfers between devices: 27.5 us -> 0.01 us  [on_device(): value_piece = lax.all_gather(value_rows, 'ctx', axis=0, tiled=True)]
    unnamed x15 -> x14, waiting for transfers between devices: 58.9 us -> 58.2 us
  transfers between devices with their start and end apart: 13 -> 15, of which waited for: 12 -> 12; matrix products, arithmetic and copies ran while one was open for 4% -> 5% of each run, Pallas kernels for 0% -> 0%
where the time goes in v1:
time: 2540 us; the launch traced here: 2530 us
  waiting for transfers between devices  2160 us (85%)
  matrix products  147 us (6%)
  blocking collectives  86 us (3%)
  other arithmetic  57.1 us (2%)
  local copies, waits for them, and re-layouts  52 us (2%)
    reduce_scatter x1, waiting for transfers between devices, on_device(): lax.psum_scatter(grad_proj.astype(jnp.bfloat16), 'fsdp', scatter_dimensio...  343 us
    reduce_scatter x1, waiting for transfers between devices, on_device(): lax.psum_scatter(grad_fc.astype(jnp.bfloat16), 'fsdp', scatter_dimension=...  343 us
    all_gather x1, waiting for transfers between devices, on_device(): lax.all_gather(proj_weight, 'fsdp', axis=1, tiled=True)  336 us
    all_gather x1, waiting for transfers between devices, on_device(): lax.all_gather(fc_weight, 'fsdp', axis=0, tiled=True)  296 us
    reduce_scatter x1, waiting for transfers between devices, on_device(): lax.psum_scatter(grad_qkv.astype(jnp.bfloat16), 'fsdp', scatter_dimension...  263 us
    all_gather x1, waiting for transfers between devices, on_device(): lax.all_gather(qkv_weight, 'fsdp', axis=0, tiled=True)  226 us
    psum x1, waiting for transfers between devices, on_device(): lax.psum(attn_parts[2].astype(jnp.bfloat16), 'ctx').astype(jnp.float32)  157 us
    ppermute x2, waiting for transfers between devices, ring_gather(): lax.ppermute(going_up, axis, [(d, (d + 1) % ways) for d in range(ways)])  64.2 us
  transfers between devices with their start and end apart: 15, of which 12 were waited for; matrix products, arithmetic and copies ran while one was open for 5% of the time, Pallas kernels for 0%

profile of v1, /device:TPU:0, one launch (start us, length us, event | category | flops | bytes accessed | tf_op | source)
XLA Modules:
  0.0 2530.8 jit_solution(7717829114070762614)
XLA Ops:
  10.0 13.5 all-gather
  25.2 28.7 %all-reduce.17 = (bf16[1600]{0:T(1024)(128)(2,1)S(1)}, bf16[1600]{0:T(1024)(128)(2,1)S(1)}, bf16[1600]{0:T(1024)(128)(2,1)S(1)}, bf16[6400]{0:T(1024)(128)(2,1)S...) all-reduce(bf16[1600]{0:T(1024)(128)(2,1)S(1)} %dynamic-update-slic, ...), channel_id=1, replica_groups=mesh['ctx'=8,'fsdp'=4] {'fsdp'}, use_global_device_ids=true, to_apply=%add.1 | all-reduce | flops 14400 | bytes 57600
  54.5 226.2 %all-gather.7.cloned.1.call-done = bf16[1600,4800]{1,0:T(8,128)(2,1)} async-done(((bf16[400,4800]{1,0:T(8,128)(2,1)}), bf16[1600,4800]{1,0:T(8,128)(2,1)}) %all-gather.7.cloned.1.call-update) | async-done | bytes 15360016 | tf_op jit(solution)/shard_map/all_gather | solution.py:87
  280.8 12.3 fusion.80
  302.8 30.4 %collective-permute-done = bf16[400,1600]{1,0:T(8,128)(2,1)} collective-permute-done((bf16[400,1600]{1,0:T(8,128)(2,1)}, bf16[400,1600]{1,0:T(8,128)(2,1)}, u32[]{:S(2)}, u32[]{:S(2)}) %collective-permute-start) | collective-permute-done | bytes 1280032 | tf_op jit(solution)/shard_map/ppermute | solution.py:18
  341.7 17.4 collective-permute-done.1
  361.6 33.8 %collective-permute-done.2 = bf16[400,1600]{1,0:T(8,128)(2,1)} collective-permute-done((bf16[400,1600]{1,0:T(8,128)(2,1)}, bf16[400,1600]{1,0:T(8,128)(2,1)}, u32[]{:S(2)}, u32[]{:S(2)}) %collective-permute-start.2) | collective-permute-done | bytes 1280032 | tf_op jit(solution)/shard_map/ppermute | solution.py:18
  397.9 20.2 while.34
  423.4 295.9 %all-gather.13.cloned.1.call-done = bf16[1600,6400]{1,0:T(8,128)(2,1)} async-done(((bf16[400,6400]{1,0:T(8,128)(2,1)}), bf16[1600,6400]{1,0:T(8,128)(2,1)}) %all-gather.13.cloned.1.call-update) | async-done | bytes 20480016 | tf_op jit(solution)/shard_map/all_gather | solution.py:93
  719.3 12.4 convolution_add_fusion
  731.7 336.1 %all-gather.15.cloned.1.call-done = bf16[6400,1600]{0,1:T(8,128)(2,1)} async-done(((bf16[6400,400]{0,1:T(8,128)(2,1)}), bf16[6400,1600]{0,1:T(8,128)(2,1)}) %all-gather.15.cloned.1.call-update) | async-done | bytes 20480016 | tf_op jit(solution)/shard_map/all_gather | solution.py:95
  1067.9 13.8 fusion.89
  1081.7 12.7 multiply_reduce_fusion
  1106.4 38.6 %while.35 = (s32[]{:T(128)}, f32[128,25,64]{0,2,1:T(8,128)S(1)}, f32[1024,3200]{0,1:T(8,128)}, bf16[1024,1600]{0,1:T(8,128)(2,1)}, bf16[128,25,64]{0,2,1:T(8,128...) while((s32[]{:T(128)}, f32[128,25,64]{0,2,1:T(8,128)S(1)}, ...), condition=%wide.region_12.13_spmd.clone, body=%wide.region_11.12_spmd.clone.sunk | while | flops 1291739776 | bytes 84286680 | solution.py:57
  1168.6 56.4 %reduce-scatter.19.cloned.1.call-done = bf16[128,3200]{1,0:T(8,128)(2,1)} async-done(((bf16[1024,3200]{1,0:T(8,128)(2,1)}), bf16[128,3200]{1,0:T(8,128)(2,1)}) %reduce-scatter.19.cloned.1.call-update) | async-done | bytes 819216
  1236.2 11.7 convolution_convert_fusion
  1262.7 60.4 %reduce-scatter.13.cloned.1.call-done = bf16[400,1600]{1,0:T(8,128)(2,1)} async-done(((bf16[1600,1600]{1,0:T(8,128)(2,1)}), bf16[400,1600]{1,0:T(8,128)(2,1)}) %reduce-scatter.13.cloned.1.call-update) | async-done | bytes 1280016 | tf_op jit(solution)/shard_map/reduce_scatter | solution.py:280
  1323.2 263.4 %reduce-scatter.11.cloned.1.call-done = bf16[400,4800]{1,0:T(8,128)(2,1)} async-done(((bf16[1600,4800]{1,0:T(8,128)(2,1)}), bf16[400,4800]{1,0:T(8,128)(2,1)}) %reduce-scatter.11.cloned.1.call-update) | async-done | bytes 3840016 | tf_op jit(solution)/shard_map/reduce_scatter | solution.py:274
  1586.6 343.1 %reduce-scatter.17.cloned.1.call-done = bf16[6400,400]{0,1:T(8,128)(2,1)} async-done(((bf16[6400,1600]{0,1:T(8,128)(2,1)}), bf16[6400,400]{0,1:T(8,128)(2,1)}) %reduce-scatter.17.cloned.1.call-update) | async-done | bytes 5120016 | tf_op jit(solution)/shard_map/reduce_scatter | solution.py:187
  1929.7 343.1 %reduce-scatter.15.cloned.1.call-done = bf16[400,6400]{1,0:T(8,128)(2,1)} async-done(((bf16[1600,6400]{1,0:T(8,128)(2,1)}), bf16[400,6400]{1,0:T(8,128)(2,1)}) %reduce-scatter.15.cloned.1.call-update) | async-done | bytes 5120016 | tf_op jit(solution)/shard_map/reduce_scatter | solution.py:181
  2285.2 19.8 all-reduce.16
  2308.1 11.6 fusion.50
  2320.8 24.0 all-reduce.14
  2349.4 156.9 %all-reduce.20.cloned.1.call-done = (bf16[400,4800]{1,0:T(8,128)(2,1)}, bf16[400,1600]{1,0:T(8,128)(2,1)}, bf16[400,6400]{1,0:T(8,128)(2,1)}, bf16[6400,400]{0,1:T(8,128)(2,1)}) async-done(((bf16[400,4800]{1,0:T(8,128)(2,1)}, bf16[400,1600]{1,0:T(8,128)(2,1)}, bf16[400,6400]{1,0:T(8,128)(2,1)}, bf16[6400,400]{0,1:T(8,128)(2,1)}), (bf16[400,4800]{1,0:T(8,128)(2,1)}, bf16[400,1600]{1,0:T(8,128)(2,1)}, ...) | async-done | bytes 15360016 | tf_op jit(solution)/shard_map/psum | solution.py:290
  (276 shorter events, 188.8 us)
Async XLA Ops:
  7.3 273.5 %all-gather.7.cloned.1.call-start = ((), (), s32[]{:S(2)}) async-start(), calls=%async_computation.6 | async-start | bytes 19456000 | tf_op jit(solution)/shard_map/all_gather | solution.py:87
  8.0 389.8 %all-gather.11.cloned.1.call-start = ((), (), s32[]{:S(2)}) async-start(), calls=%async_computation.8 | async-start | bytes 3686400 | tf_op jit(solution)/shard_map/all_gather | solution.py:126
  54.0 239.1 %copy-start.26 = (f32[1600]{0:T(1024)}, f32[1600]{0:T(1024)S(1)}, u32[]{:S(2)}) copy-start(f32[1600]{0:T(1024)S(1)} %convert_element_type.234) | copy-start | bytes 19204
  54.0 239.1 %copy-start.22 = (f32[1600]{0:T(1024)}, f32[1600]{0:T(1024)S(1)}, u32[]{:S(2)}) copy-start(f32[1600]{0:T(1024)S(1)} %convert_element_type.233) | copy-start | bytes 19204
  54.3 238.8 %copy-start.32 = (f32[128]{0:T(128)}, f32[128]{0:T(128)S(1)}, u32[]{:S(2)}) copy-start(f32[128]{0:T(128)S(1)} %broadcast_multiply_fusion.1) | copy-start | bytes 1540
  295.7 102.1 %all-gather.9.cloned.1.call-start = ((), (), s32[]{:S(2)}) async-start(), calls=%async_computation.7 | async-start | bytes 3686400 | tf_op jit(solution)/shard_map/all_gather | solution.py:125
  297.7 421.6 %all-gather.13.cloned.1.call-start = ((), (), s32[]{:S(2)}) async-start(), calls=%async_computation.9 | async-start | bytes 25600000 | tf_op jit(solution)/shard_map/all_gather | solution.py:93
  298.3 769.5 %all-gather.15.cloned.1.call-start = ((), (), s32[]{:S(2)}) async-start(), calls=%async_computation.10 | async-start | bytes 25600000 | tf_op jit(solution)/shard_map/all_gather | solution.py:95
  298.9 926.0 %reduce-scatter.19.cloned.1.call-start = ((), (), s32[]{:S(2)}) async-start(), calls=%async_computation.15 | async-start | bytes 7372800
  298.9 34.3 %collective-permute-start = (bf16[400,1600]{1,0:T(8,128)(2,1)}, bf16[400,1600]{1,0:T(8,128)(2,1)}, u32[]{:S(2)}, u32[]{:S(2)}) collective-permute-start(bf16[400,1600]{1,0:T(8,128)(2,1)} %param.24), channel_id=1, source_target_pairs={{0,1},{1,2},{2,3},{3,0},{4,5},{5,6},{6,7},{7,4},{8,9},{9,10},{10,1... | collective-permute-start | bytes 3840008 | tf_op jit(solution)/shard_map/ppermute | solution.py:18
  299.0 60.1 %collective-permute-start.1 = (bf16[400,1600]{1,0:T(8,128)(2,1)}, bf16[400,1600]{1,0:T(8,128)(2,1)}, u32[]{:S(2)}, u32[]{:S(2)}) collective-permute-start(bf16[400,1600]{1,0:T(8,128)(2,1)} %param.24), channel_id=1, source_target_pairs={{0,3},{1,0},{2,1},{3,2},{4,7},{5,4},{6,5},{7,6},{8,11},{9,8},{10,9... | collective-permute-start | bytes 3840008 | tf_op jit(solution)/shard_map/ppermute | solution.py:21
  333.2 62.1 %collective-permute-start.2 = (bf16[400,1600]{1,0:T(8,128)(2,1)}, bf16[400,1600]{1,0:T(8,128)(2,1)}, u32[]{:S(2)}, u32[]{:S(2)}) collective-permute-start(bf16[400,1600]{1,0:T(8,128)(2,1)} %collective-permute-done), channel_id=1, source_target_pairs={{0,1},{1,2},{2,3},{3,0},{4,5},{5,6},{6,7},{7,4},{8,9},{9,10},{10,1... | collective-permute-start | bytes 3840008 | tf_op jit(solution)/shard_map/ppermute | solution.py:18
  333.8 760.6 %copy-start.20 = (f32[1600]{0:T(1024)}, f32[1600]{0:T(1024)S(1)}, u32[]{:S(2)}) copy-start(f32[1600]{0:T(1024)S(1)} %convert_element_type.242) | copy-start | bytes 19204
  333.8 385.5 %copy-start.24 = (f32[1600]{0:T(1024)}, f32[1600]{0:T(1024)S(1)}, u32[]{:S(2)}) copy-start(f32[1600]{0:T(1024)S(1)} %convert_element_type.243) | copy-start | bytes 19204
  423.1 671.3 %copy-start = (f32[128,1600]{0,1:T(8,128)}, f32[128,1600]{0,1:T(8,128)S(1)}, u32[]{:S(2)}) copy-start(f32[128,1600]{0,1:T(8,128)S(1)} %get-tuple-element.486) | copy-start | bytes 2457604
  423.1 671.3 %copy-start.28 = (f32[128]{0:T(128)}, f32[128]{0:T(128)S(1)}, u32[]{:S(2)}) copy-start(f32[128]{0:T(128)S(1)} %broadcast_multiply_fusion) | copy-start | bytes 1540
  423.4 671.0 %copy-start.30 = (f32[128]{0:T(128)}, f32[128]{0:T(128)S(1)}, u32[]{:S(2)}) copy-start(f32[128]{0:T(128)S(1)} %fusion.76) | copy-start | bytes 1540
  423.4 644.5 %copy-start.6 = (bf16[1,128,1600]{1,2,0:T(8,128)(2,1)S(1)}, bf16[1,128,1600]{1,2,0:T(8,128)(2,1)}, u32[]{:S(2)}) copy-start(bf16[1,128,1600]{1,2,0:T(8,128)(2,1)} %param.19) | copy-start | bytes 1228804
  1163.1 160.1 %reduce-scatter.13.cloned.1.call-start = ((), (), s32[]{:S(2)}) async-start(), calls=%async_computation.12 | async-start | bytes 6656000 | tf_op jit(solution)/shard_map/reduce_scatter | solution.py:280
  1168.2 418.4 %reduce-scatter.11.cloned.1.call-start = ((), (), s32[]{:S(2)}) async-start(), calls=%async_computation.11 | async-start | bytes 19456000 | tf_op jit(solution)/shard_map/reduce_scatter | solution.py:274
  1235.2 694.4 %reduce-scatter.17.cloned.1.call-start = ((), (), s32[]{:S(2)}) async-start(), calls=%async_computation.14 | async-start | bytes 25600000 | tf_op jit(solution)/shard_map/reduce_scatter | solution.py:187
  1248.0 1024.8 %reduce-scatter.15.cloned.1.call-start = ((), (), s32[]{:S(2)}) async-start(), calls=%async_computation.13 | async-start | bytes 25600000 | tf_op jit(solution)/shard_map/reduce_scatter | solution.py:181
  1260.1 1059.7 %reduce-scatter.21.cloned.1.call-start = ((), (), s32[]{:S(2)}) async-start(), calls=%async_computation.16 | async-start | bytes 512000
  1262.5 1243.8 %all-reduce.20.cloned.1.call-start = ((), (), s32[]{:S(2)}) async-start(), calls=%async_computation.17 | async-start | bytes 30924800 | tf_op jit(solution)/shard_map/psum | solution.py:290
  (46 other events, 1178.0 us)
Sparse Core Ops, SparseCore 0:
  9.7 271.0 all-gather.6
  295.8 31.6 all-gather.10
  330.0 33.3 all-gather.8
  364.9 354.3 all-gather.12
  720.7 347.0 all-gather.14
  1163.2 61.6 reduce-scatter.18
  1227.9 95.2 reduce-scatter.12
  1325.7 260.8 reduce-scatter.10
  1588.9 340.6 reduce-scatter.16
  1932.0 340.7 reduce-scatter.14
  2275.6 22.2 reduce-scatter.20
  2302.4 203.7 all-reduce.19
